TPU v7x, 256 devices: a whole 4x4x8 slice. The times are simulated.
256 devices in a mesh: row: 32 (over y, z), col: 8 (over x, core).
Axes of the slice: x: 4, y: 4, z: 8, core: 2. Of those that a mesh axis runs over, the one named last changes fastest.
Arguments:
- diag_block: float32 [256, 256], P(('row', 'col')), may hold values from -1 to 40, as said below
- panel: float32 [24576, 256], P(('row', 'col')), may hold values from -6 to 6
- trailing: bfloat16 [24576, 24576], P('row', 'col'), may hold values from -6 to 6
Outputs:
- diag_factor: float32 [256, 256], P(('row', 'col'))
- panel_factor: float32 [24576, 256], P(('row', 'col'))
- trailing_out: bfloat16 [24576, 24576], P('row', 'col')
Inputs may be any that keep to these rules, and one draw needn't show every extreme that they name: diag_block is symmetric, with off-diagonal entries in -1 to 1 and diagonal entries in 24 to 40, so it is positive definite.
All inputs are finite; a program needn't handle non-finite values.
Results may differ from a plain program's by a relative error of at most 0.001.
Values sent between devices are 32-bit elements; how exact they have to be, the bound alone decides.
No kernel may reach another device: no remote copies, remote signals or barrier semaphores. Data moves between devices by JAX's collectives and lax.ppermute only.
A program may use at most 128 MiB of HBM per device.

v0:
```python
import jax
import jax.numpy as jnp
from jax import lax
from jax.sharding import PartitionSpec as P

BLOCK = 256
GRID = ("row", "col")
HIGHEST = lax.Precision.HIGHEST
HIGH = lax.Precision.HIGH


def product(a, b, precision=HIGHEST):
    return jnp.dot(a, b, precision=precision, preferred_element_type=jnp.float32)


def per_device(diag_block, panel, trailing):
    count_rows, count_cols = (lax.axis_size("row"), lax.axis_size("col"))
    devices = count_rows * count_cols
    ratio = count_rows // count_cols
    panel_width = panel.shape[1]
    swap = [
        ((r * count_cols + a) * count_cols + b, (r * count_cols + b) * count_cols + a)
        for r in range(ratio)
        for a in range(count_cols)
        for b in range(count_cols)
    ]
    moved = lax.ppermute(panel, GRID, swap)
    column_rows = lax.all_gather(moved, "row", axis=0, tiled=True)
    diag_share = diag_block.shape[0]
    copies = jnp.broadcast_to(diag_block[None], (devices,) + diag_block.shape)
    copies = copies.reshape(devices * diag_share, panel_width)
    whole_diag = lax.all_to_all(copies, GRID, 0, 0, tiled=True)
    row_rows = lax.all_gather(panel, "col", axis=0, tiled=True)
    diag_factor = jnp.linalg.cholesky(whole_diag)
    identity = jnp.eye(panel_width, dtype=jnp.float32)
    inverse = lax.linalg.triangular_solve(diag_factor, identity, left_side=True, lower=True)
    panel_factor = product(panel, inverse.T)
    factor_rows = lax.dynamic_slice_in_dim(
        diag_factor, lax.axis_index(GRID) * diag_share, diag_share, 0
    )
    left = product(product(row_rows, inverse.T), inverse)
    per_block = row_rows.shape[0] // BLOCK
    grouped = column_rows.reshape(ratio, per_block, BLOCK, panel_width)
    right = jnp.transpose(grouped, (1, 0, 2, 3)).reshape(-1, panel_width)
    update = product(left, right.T, HIGH)
    trailing_out = (trailing.astype(jnp.float32) - update).astype(jnp.bfloat16)
    return (factor_rows, panel_factor, trailing_out)


def solution(mesh):
    placed = (P(GRID, None), P(GRID, None), P("row", "col"))
    return jax.shard_map(per_device, mesh=mesh, in_specs=placed, out_specs=placed, check_vma=False)
```

profile of v0, /device:TPU:1, one launch (start us, length us, event | category | flops | bytes accessed | tf_op | source)
XLA Modules:
  0.0 135.2 jit_solution(17759163634431748561)
XLA Ops:
  7.2 0.0 copy-start
  7.2 0.0 all-gather.2.cloned.1.call-start
  7.2 4.9 %collective-permute-start = (f32[96,256]{1,0:T(8,128)}, f32[96,256]{1,0:T(8,128)S(1)}, u32[]{:S(2)}, u32[]{:S(2)}) collective-permute-start(f32[96,256]{1,0:T(8,128)} %param.4), channel_id=1, source_target_pairs={{0,0},{1,8},{2,16},{3,24},{4,32},{5,40},{6,48},{7,56},{8,1},{9,9},... | collective-permute-start | bytes 294920 | tf_op jit(solution)/shard_map/ppermute | solution.py:27
  12.2 2.5 %collective-permute-done = f32[96,256]{1,0:T(8,128)S(1)} collective-permute-done((f32[96,256]{1,0:T(8,128)}, f32[96,256]{1,0:T(8,128)S(1)}, u32[]{:S(2)}, u32[]{:S(2)}) %collective-permute-start) | collective-permute-done | bytes 98336 | tf_op jit(solution)/shard_map/ppermute | solution.py:27
  14.7 0.0 copy-start.1
  14.7 0.6 copy-done.1
  15.3 0.0 all-gather.2.cloned.1.call-update
  15.3 1.5 %reshape.41 = f32[256,1,256]{2,1,0:T(1,128)} broadcast(f32[256]{0:T(256)} %bitcast.49), dimensions={2} | broadcast | bytes 263168 | tf_op jit(solution)/shard_map/reshape | solution.py:31
  16.8 20.7 %all-to-all-start = ((f32[256,1,256]{2,1,0:T(1,128)}), f32[256,1,256]{2,1,0:T(1,128)S(1)}, u32[]{:S(2)}, u32[]{:S(2)}) async-start(f32[256,1,256]{2,1,0:T(1,128)} %reshape.41), calls=%async_computation | async-start | bytes 524288 | tf_op jit(solution)/shard_map/all_to_all | solution.py:32
  37.6 16.0 %all_gather.6 = f32[768,256]{1,0:T(8,128)S(1)} all-gather(f32[96,256]{1,0:T(8,128)} %param.4), channel_id=1, replica_groups=mesh['row'=32,'col'=8] {'col'}, dimensions={0}, use_global_device_ids=true | all-gather | bytes 884736 | tf_op jit(solution)/shard_map/all_gather | solution.py:33
  53.6 0.5 all-to-all-done
  54.1 0.1 copy.10
  54.3 11.7 %cholesky.50 = f32[128,128]{1,0:T(8,128)S(1)} custom-call(f32[128,128]{1,0:T(8,128)S(1)} %cholesky.118), custom_call_target="Cholesky" | custom-call | tf_op jit(solution)/shard_map/jit(cholesky)/cholesky | solution.py:34
  66.1 9.8 %custom-call.14 = f32[1,128,128]{1,2,0:T(8,128)S(1)} custom-call(f32[1,128,128]{2,1,0:T(8,128)S(1)} %get-tuple-element.26), custom_call_target="InvertDiagBlocksLowerTriangular" | custom-call | tf_op jit(solution)/shard_map/jit(cholesky)/cholesky | solution.py:34
  75.9 0.2 constant_dynamic-update-slice_fusion
  76.1 0.3 convolution_subtract_fusion.1
  76.4 11.7 %cholesky.105 = f32[128,128]{1,0:T(8,128)S(1)} custom-call(f32[128,128]{1,0:T(8,128)S(1)} %convolution_subtract_fusion.1), custom_call_target="Cholesky" | custom-call | tf_op jit(solution)/shard_map/jit(cholesky)/cholesky | solution.py:34
  88.1 0.6 compare_reduce_fusion
  90.1 0.1 triangular_solve.44
  90.2 4.1 %while.1 = (s32[]{:T(128)}, f32[256,256]{1,0:T(8,128)S(1)}, s32[2,2]{1,0:T(2,128)S(1)}, f32[2,128,128]{2,1,0:T(8,128)S(1)}, s32[]{:T(128)}) while((s32[]{:T(128)}, f32[256,256]{1,0:T(8,128)S(1)}, s32[2,2]{1,0:T(2,128)S(1)}, f32[2,128,128]{2,1,0:T(8,128)S(1)}, s32[]{:T(128)}) %tuple.28), condition=%wide.while_cond, body=%wide.while_body.sunk | while | flops 2 | bytes 131189 | solution.py:36
  90.3 0.6 fusion.25
  90.9 1.4 %bitcast_dynamic-update-slice_fusion.2 = f32[2,128,128]{2,1,0:T(8,128)S(1)} fusion(f32[2,128,128]{2,1,0:T(8,128)S(1)} %get-tuple-element.68, s32[]{:T(128)S(6)} %copy.20, f32[256,256]{1,0:T(8,128)S(1)} %get-tuple-element.71, s32[]{:T(128)} %bitcast.45, s32[]{:T(128)} %bitcast.46), kind=kLoop, calls=%fused_computation.clone.1 | loop fusion | bytes 131084 | tf_op jit(solution)/shard_map/triangular_solve
  92.3 0.6 fusion.25
  92.9 1.4 %bitcast_dynamic-update-slice_fusion.2 = f32[2,128,128]{2,1,0:T(8,128)S(1)} fusion(f32[2,128,128]{2,1,0:T(8,128)S(1)} %get-tuple-element.68, s32[]{:T(128)S(6)} %copy.20, f32[256,256]{1,0:T(8,128)S(1)} %get-tuple-element.71, s32[]{:T(128)} %bitcast.45, s32[]{:T(128)} %bitcast.46), kind=kLoop, calls=%fused_computation.clone.1 | loop fusion | bytes 131084 | tf_op jit(solution)/shard_map/triangular_solve
  94.3 19.7 %custom-call.15 = f32[2,128,128]{1,2,0:T(8,128)S(1)} custom-call(f32[2,128,128]{2,1,0:T(8,128)S(1)} %get-tuple-element.10), custom_call_target="InvertDiagBlocksLowerTriangular" | custom-call | tf_op jit(solution)/shard_map/triangular_solve | solution.py:36
  114.0 0.6 constant_dynamic-slice_fusion.1
  114.6 0.3 fusion.4
  114.9 0.3 convolution_subtract_fusion
  115.1 0.3 fusion.7
  115.4 0.0 copy-done
  115.4 1.0 convolution_bitcast_fusion
  116.5 0.8 fusion.3
  117.3 1.4 %fusion.2 = f32[768,256]{1,0:T(8,128)S(1)} fusion(f32[256,768]{1,0:T(8,128)S(1)} %fusion.3, f32[128,256]{1,0:T(8,128)S(1)} %fusion.7, f32[128,256]{1,0:T(8,128)S(1)} %fusion.4), kind=kOutput, calls=%fused_computation.13 | convolution fusion | flops 604045312 | bytes 1835008 | tf_op jit(solution)/shard_map/dot_general | solution.py:13
  118.8 0.0 all-gather.2.cloned.1.call-done
  118.8 2.1 %copy.12 = f32[3,4,256,256]{3,2,1,0:T(8,128)S(1)} copy(f32[3,4,256,256]{3,2,0,1:T(8,128)} %bitcast.48) | data formatting | bytes 6291456 | tf_op jit(solution)/shard_map/transpose | solution.py:44
  120.9 7.5 %subtract_convert_fusion = bf16[768,3072]{1,0:T(8,128)(2,1)} fusion(bf16[768,3072]{1,0:T(8,128)(2,1)} %param.5, f32[768,256]{1,0:T(8,128)S(1)} %fusion.2, f32[3072,256]{1,0:T(8,128)S(1)} %bitcast.47), kind=kOutput, calls=%fused_computation.2 | convolution fusion | flops 3630956544 | bytes 13369344 | tf_op jit(solution)/shard_map/dot_general | solution.py:13
  (11 shorter events, 0.2 us)
Async XLA Ops:
  7.2 108.3 %copy-start = (f32[96,256]{1,0:T(8,128)S(1)}, f32[96,256]{1,0:T(8,128)}, u32[]{:S(2)}) copy-start(f32[96,256]{1,0:T(8,128)} %param.4) | copy-start | bytes 294916
  7.2 111.6 %all-gather.2.cloned.1.call-start = ((), (), s32[]{:S(2)}) async-start(), calls=%async_computation.1 | async-start | bytes 3244032 | tf_op jit(solution)/shard_map/all_gather | solution.py:28
  7.2 7.4 %collective-permute-start = (f32[96,256]{1,0:T(8,128)}, f32[96,256]{1,0:T(8,128)S(1)}, u32[]{:S(2)}, u32[]{:S(2)}) collective-permute-start(f32[96,256]{1,0:T(8,128)} %param.4), channel_id=1, source_target_pairs={{0,0},{1,8},{2,16},{3,24},{4,32},{5,40},{6,48},{7,56},{8,1},{9,9},... | collective-permute-start | bytes 294920 | tf_op jit(solution)/shard_map/ppermute | solution.py:27
  14.7 0.6 copy-start.1
  16.8 37.3 %all-to-all-start = ((f32[256,1,256]{2,1,0:T(1,128)}), f32[256,1,256]{2,1,0:T(1,128)S(1)}, u32[]{:S(2)}, u32[]{:S(2)}) async-start(f32[256,1,256]{2,1,0:T(1,128)} %reshape.41), calls=%async_computation | async-start | bytes 524288 | tf_op jit(solution)/shard_map/all_to_all | solution.py:32
Sparse Core Ops, SparseCore 0:
  15.4 85.1 all-gather.1
where the time goes:
time: 136 us; the launch traced here: 135 us
  other arithmetic  53.7 us (39%)
  starting transfers between devices  25.7 us (19%)
  blocking collectives  16 us (12%)
  between operations  15.5 us (11%)
  matrix products  12.1 us (9%)
  local copies, waits for them, and re-layouts  9.01 us (7%)
  waiting for transfers between devices  3.02 us (2%)
    another operation x6, other arithmetic, per_device(): diag_factor = jnp.linalg.cholesky(whole_diag)  34 us
    all_to_all x1, starting transfers between devices, per_device(): whole_diag = lax.all_to_all(copies, GRID, 0, 0, tiled=True)  20.7 us
    another operation x3, other arithmetic, per_device(): lax.linalg.triangular_solve(diag_factor, identity, left_side=True, lower=...  19.7 us
    all_gather x1, blocking collectives, per_device(): row_rows = lax.all_gather(panel, 'col', axis=0, tiled=True)  16 us
    dot_general x4, matrix products, product(): jnp.dot(a, b, precision=precision, preferred_element_type=jnp.float32)  10.8 us
    ppermute x1, starting transfers between devices, per_device(): moved = lax.ppermute(panel, GRID, swap)  4.93 us
    another operation x6, local copies, waits for them, and re-layouts  3.95 us
  transfers between devices with their start and end apart: 3, of which 2 were waited for; matrix products, arithmetic and copies ran while one was open for 48% of the time, Pallas kernels for 0%

commit v1 on v0

--- a/solution.py
+++ b/solution.py
@@ -7,6 +7,11 @@
 GRID = ("row", "col")
 HIGHEST = lax.Precision.HIGHEST
 HIGH = lax.Precision.HIGH
+
+
+def all_by_exchange(x, mesh_axis, d):
+    stack = jnp.stack([x] * lax.axis_size(mesh_axis))
+    return jnp.concatenate(lax.all_to_all(stack, mesh_axis, 0, 0), axis=d)
 
 
 def product(a, b, precision=HIGHEST):
@@ -30,7 +35,7 @@
     copies = jnp.broadcast_to(diag_block[None], (devices,) + diag_block.shape)
     copies = copies.reshape(devices * diag_share, panel_width)
     whole_diag = lax.all_to_all(copies, GRID, 0, 0, tiled=True)
-    row_rows = lax.all_gather(panel, "col", axis=0, tiled=True)
+    row_rows = all_by_exchange(panel, "col", 0)
     diag_factor = jnp.linalg.cholesky(whole_diag)
     identity = jnp.eye(panel_width, dtype=jnp.float32)
     inverse = lax.linalg.triangular_solve(diag_factor, identity, left_side=True, lower=True)

time: 136 us -> 141 us (1.037)
  blocking collectives: 16 us -> 0 us
  waiting for transfers between devices: 3.02 us -> 19 us
  starting transfers between devices: 25.7 us -> 29.5 us
  local copies, waits for them, and re-layouts: 9.01 us -> 10.9 us
    all_to_all x1, waiting for transfers between devices: 0.49 us -> 16.5 us  [per_device(): whole_diag = lax.all_to_all(copies, GRID, 0, 0, tiled=True)]
    all_gather x1 -> x0, blocking collectives: 16 us -> none  [per_device(): row_rows = lax.all_gather(panel, 'col', axis=0, tiled=True)]
    all_to_all x0 -> x1, starting transfers between devices: none -> 3.82 us  [all_by_exchange(): return jnp.concatenate(lax.all_to_all(stack, mesh_axis, 0, 0), axis=d)]
    another operation x6 -> x7, local copies, waits for them, and re-layouts: 3.95 us -> 5.8 us
  transfers between devices with their start and end apart: 3 -> 4, of which waited for: 2 -> 2; matrix products, arithmetic and copies ran while one was open for 48% -> 47% of each run, Pallas kernels for 0% -> 0%
where the time goes in v1:
time: 141 us
  other arithmetic  53.9 us (38%)
  starting transfers between devices  29.5 us (21%)
  waiting for transfers between devices  19 us (13%)
  between operations  15.5 us (11%)
  matrix products  12.1 us (9%)
  local copies, waits for them, and re-layouts  10.9 us (8%)
    another operation x6, other arithmetic, per_device(): diag_factor = jnp.linalg.cholesky(whole_diag)  34 us
    all_to_all x1, starting transfers between devices, per_device(): whole_diag = lax.all_to_all(copies, GRID, 0, 0, tiled=True)  20.7 us
    another operation x3, other arithmetic, per_device(): lax.linalg.triangular_solve(diag_factor, identity, left_side=True, lower=...  19.9 us
    all_to_all x1, waiting for transfers between devices, per_device(): whole_diag = lax.all_to_all(copies, GRID, 0, 0, tiled=True)  16.5 us
    dot_general x4, matrix products, product(): jnp.dot(a, b, precision=precision, preferred_element_type=jnp.float32)  10.8 us
    ppermute x1, starting transfers between devices, per_device(): moved = lax.ppermute(panel, GRID, swap)  4.93 us
    another operation x6, local copies, waits for them, and re-layouts  3.96 us
    all_to_all x1, starting transfers between devices, all_by_exchange(): return jnp.concatenate(lax.all_to_all(stack, mesh_axis, 0, 0), axis=d)  3.82 us
  transfers between devices with their start and end apart: 4, of which 2 were waited for; matrix products, arithmetic and copies ran while one was open for 47% of the time, Pallas kernels for 0%

profile of v1, /device:TPU:1, one launch (start us, length us, event | category | flops | bytes accessed | tf_op | source)
XLA Modules:
  0.0 140.9 jit_solution(3135027421657996628)
XLA Ops:
  7.2 0.0 copy-start
  7.2 0.0 all-gather.2.cloned.1.call-start
  7.2 4.9 %collective-permute-start = (f32[96,256]{1,0:T(8,128)}, f32[96,256]{1,0:T(8,128)S(1)}, u32[]{:S(2)}, u32[]{:S(2)}) collective-permute-start(f32[96,256]{1,0:T(8,128)} %param.4), channel_id=1, source_target_pairs={{0,0},{1,8},{2,16},{3,24},{4,32},{5,40},{6,48},{7,56},{8,1},{9,9},... | collective-permute-start | bytes 294920 | tf_op jit(solution)/shard_map/ppermute | solution.py:32
  12.2 2.5 %collective-permute-done = f32[96,256]{1,0:T(8,128)S(1)} collective-permute-done((f32[96,256]{1,0:T(8,128)}, f32[96,256]{1,0:T(8,128)S(1)}, u32[]{:S(2)}, u32[]{:S(2)}) %collective-permute-start) | collective-permute-done | bytes 98336 | tf_op jit(solution)/shard_map/ppermute | solution.py:32
  14.7 0.0 copy-start.1
  14.7 0.6 copy-done.1
  15.3 0.0 all-gather.2.cloned.1.call-update
  15.3 1.5 %reshape.46 = f32[256,1,256]{2,1,0:T(1,128)} broadcast(f32[256]{0:T(256)} %bitcast.51), dimensions={2} | broadcast | bytes 263168 | tf_op jit(solution)/shard_map/reshape | solution.py:36
  16.8 20.7 %all-to-all-start = ((f32[256,1,256]{2,1,0:T(1,128)}), f32[256,1,256]{2,1,0:T(1,128)S(1)}, u32[]{:S(2)}, u32[]{:S(2)}) async-start(f32[256,1,256]{2,1,0:T(1,128)} %reshape.46), calls=%async_computation | async-start | bytes 524288 | tf_op jit(solution)/shard_map/all_to_all | solution.py:37
  37.6 16.5 %all-to-all-done = f32[256,1,256]{2,1,0:T(1,128)S(1)} async-done(((f32[256,1,256]{2,1,0:T(1,128)}), f32[256,1,256]{2,1,0:T(1,128)S(1)}, u32[]{:S(2)}, u32[]{:S(2)}) %all-to-all-start) | async-done | bytes 262176 | tf_op jit(solution)/shard_map/all_to_all | solution.py:37
  54.1 1.8 %stack.2 = f32[8,96,256]{2,1,0:T(8,128)} broadcast(f32[96,256]{1,0:T(8,128)} %param.4), dimensions={1,2} | broadcast | bytes 884736 | tf_op jit(solution)/shard_map/stack | solution.py:13
  55.9 3.8 %all-to-all-start.1 = ((f32[8,96,256]{2,1,0:T(8,128)}), f32[8,96,256]{2,1,0:T(8,128)S(1)}, u32[]{:S(2)}, u32[]{:S(2)}) async-start(f32[8,96,256]{2,1,0:T(8,128)} %stack.2), calls=%async_computation.1 | async-start | bytes 1572864 | tf_op jit(solution)/shard_map/all_to_all | solution.py:14
  59.8 0.1 copy.10
  60.0 11.7 %cholesky.50 = f32[128,128]{1,0:T(8,128)S(1)} custom-call(f32[128,128]{1,0:T(8,128)S(1)} %cholesky.118), custom_call_target="Cholesky" | custom-call | tf_op jit(solution)/shard_map/jit(cholesky)/cholesky | solution.py:39
  71.7 9.8 %custom-call.14 = f32[1,128,128]{1,2,0:T(8,128)S(1)} custom-call(f32[1,128,128]{2,1,0:T(8,128)S(1)} %get-tuple-element.26), custom_call_target="InvertDiagBlocksLowerTriangular" | custom-call | tf_op jit(solution)/shard_map/jit(cholesky)/cholesky | solution.py:39
  81.6 0.2 constant_dynamic-update-slice_fusion
  81.8 0.3 convolution_subtract_fusion.1
  82.0 11.7 %cholesky.105 = f32[128,128]{1,0:T(8,128)S(1)} custom-call(f32[128,128]{1,0:T(8,128)S(1)} %convolution_subtract_fusion.1), custom_call_target="Cholesky" | custom-call | tf_op jit(solution)/shard_map/jit(cholesky)/cholesky | solution.py:39
  93.8 0.6 compare_reduce_fusion
  95.8 0.1 triangular_solve.44
  95.9 4.0 %while.1 = (s32[]{:T(128)}, f32[256,256]{1,0:T(8,128)S(1)}, s32[2,2]{1,0:T(2,128)S(1)}, f32[2,128,128]{2,1,0:T(8,128)S(1)}, s32[]{:T(128)}) while((s32[]{:T(128)}, f32[256,256]{1,0:T(8,128)S(1)}, s32[2,2]{1,0:T(2,128)S(1)}, f32[2,128,128]{2,1,0:T(8,128)S(1)}, s32[]{:T(128)}) %tuple.28), condition=%wide.while_cond, body=%wide.while_body.sunk | while | flops 2 | bytes 131189 | solution.py:41
  95.9 0.6 fusion.25
  96.4 1.4 bitcast_dynamic-update-slice_fusion.2
  97.9 0.6 fusion.25
  98.5 1.4 bitcast_dynamic-update-slice_fusion.2
  99.8 19.9 %custom-call.15 = f32[2,128,128]{1,2,0:T(8,128)S(1)} custom-call(f32[2,128,128]{2,1,0:T(8,128)S(1)} %get-tuple-element.10), custom_call_target="InvertDiagBlocksLowerTriangular" | custom-call | tf_op jit(solution)/shard_map/triangular_solve | solution.py:41
  119.7 0.6 constant_dynamic-slice_fusion.1
  120.3 0.3 fusion.4
  120.6 0.3 convolution_subtract_fusion
  120.8 0.3 fusion.7
  121.1 0.0 copy-done
  121.2 1.0 convolution_bitcast_fusion
  122.2 0.0 all-to-all-done.1
  122.2 0.8 fusion.3
  123.0 1.4 %fusion.2 = f32[768,256]{1,0:T(8,128)S(1)} fusion(f32[256,768]{1,0:T(8,128)S(1)} %fusion.3, f32[128,256]{1,0:T(8,128)S(1)} %fusion.7, f32[128,256]{1,0:T(8,128)S(1)} %fusion.4), kind=kOutput, calls=%fused_computation.13 | convolution fusion | flops 604045312 | bytes 1835008 | tf_op jit(solution)/shard_map/dot_general | solution.py:18
  124.5 0.0 all-gather.2.cloned.1.call-done
  124.5 2.1 %copy.12 = f32[3,4,256,256]{3,2,1,0:T(8,128)S(1)} copy(f32[3,4,256,256]{3,2,0,1:T(8,128)} %bitcast.50) | data formatting | bytes 6291456 | tf_op jit(solution)/shard_map/transpose | solution.py:49
  126.6 7.5 %subtract_convert_fusion = bf16[768,3072]{1,0:T(8,128)(2,1)} fusion(bf16[768,3072]{1,0:T(8,128)(2,1)} %param.5, f32[768,256]{1,0:T(8,128)S(1)} %fusion.2, f32[3072,256]{1,0:T(8,128)S(1)} %bitcast.48), kind=kOutput, calls=%fused_computation.2 | convolution fusion | flops 3630956544 | bytes 13369344 | tf_op jit(solution)/shard_map/dot_general | solution.py:18
  (11 shorter events, 0.2 us)
Async XLA Ops:
  7.2 114.0 %copy-start = (f32[96,256]{1,0:T(8,128)S(1)}, f32[96,256]{1,0:T(8,128)}, u32[]{:S(2)}) copy-start(f32[96,256]{1,0:T(8,128)} %param.4) | copy-start | bytes 294916
  7.2 117.3 %all-gather.2.cloned.1.call-start = ((), (), s32[]{:S(2)}) async-start(), calls=%async_computation.2 | async-start | bytes 3244032 | tf_op jit(solution)/shard_map/all_gather | solution.py:33
  7.2 7.4 %collective-permute-start = (f32[96,256]{1,0:T(8,128)}, f32[96,256]{1,0:T(8,128)S(1)}, u32[]{:S(2)}, u32[]{:S(2)}) collective-permute-start(f32[96,256]{1,0:T(8,128)} %param.4), channel_id=1, source_target_pairs={{0,0},{1,8},{2,16},{3,24},{4,32},{5,40},{6,48},{7,56},{8,1},{9,9},... | collective-permute-start | bytes 294920 | tf_op jit(solution)/shard_map/ppermute | solution.py:32
  14.7 0.6 copy-start.1
  16.8 37.3 %all-to-all-start = ((f32[256,1,256]{2,1,0:T(1,128)}), f32[256,1,256]{2,1,0:T(1,128)S(1)}, u32[]{:S(2)}, u32[]{:S(2)}) async-start(f32[256,1,256]{2,1,0:T(1,128)} %reshape.46), calls=%async_computation | async-start | bytes 524288 | tf_op jit(solution)/shard_map/all_to_all | solution.py:37
  55.9 66.2 %all-to-all-start.1 = ((f32[8,96,256]{2,1,0:T(8,128)}), f32[8,96,256]{2,1,0:T(8,128)S(1)}, u32[]{:S(2)}, u32[]{:S(2)}) async-start(f32[8,96,256]{2,1,0:T(8,128)} %stack.2), calls=%async_computation.1 | async-start | bytes 1572864 | tf_op jit(solution)/shard_map/all_to_all | solution.py:14
Sparse Core Ops, SparseCore 0:
  15.4 84.9 all-gather.1
